TPU v7x, 32 devices: a whole 2x2x4 slice. The times are simulated.
32 devices in a mesh: seq: 8 (over z, y), tp: 4 (over x, core).
Axes of the slice: x: 2, y: 2, z: 4, core: 2. Of those that a mesh axis runs over, the one named last changes fastest.
Arguments:
- tokens: bfloat16 [2048, 2560], P('seq', 'tp'), may hold values from -6 to 6
- segments: int32 [8, 256], P('seq'), may hold values from 0 to 3, never falling along the last dimension, each value on 1 to 128 neighbouring positions
- routes: int32 [2048, 6], P('seq'), may hold values from 0 to 63, all different within a row; in each aligned block of 256 rows (0 to 255, 256 to 511, ...) at most 40 rows name the same one
- page_table: int32 [8, 32], P('seq'), may hold values from 0 to 31, each once within a row
- cache_pool: bfloat16 [256, 16, 1024], P('seq', None, 'tp'), may hold values from -6 to 6
- attn_gain: float32 [2560], replicated, may hold values from 0.1 to 1.9
- w_query: bfloat16 [2560, 2048], P(None, 'tp'), may hold values from -0.125 to 0.125
- w_keyval: bfloat16 [2560, 1024], P(None, 'tp'), may hold values from -0.125 to 0.125
- w_out: bfloat16 [2048, 2560], P('tp'), may hold values from -0.125 to 0.125
- ffn_gain: float32 [2560], replicated, may hold values from 0.1 to 1.9
- w_router: bfloat16 [2560, 64], replicated, may hold values from -0.125 to 0.125
- expert_gate: bfloat16 [64, 1536, 2560], P('seq', 'tp'), may hold values from -0.125 to 0.125
- expert_up: bfloat16 [64, 1536, 2560], P('seq', 'tp'), may hold values from -0.125 to 0.125
- expert_down: bfloat16 [64, 1536, 2560], P('seq', 'tp'), may hold values from -0.15625 to 0.15625
- shared_gate: bfloat16 [1536, 2560], P('tp'), may hold values from -0.125 to 0.125
- shared_up: bfloat16 [1536, 2560], P('tp'), may hold values from -0.125 to 0.125
- shared_down: bfloat16 [1536, 2560], P('tp'), may hold values from -0.15625 to 0.15625
Outputs:
- layer_out: bfloat16 [2048, 2560], P('seq', 'tp')
- cache_out: bfloat16 [256, 16, 1024], P('seq', None, 'tp')
Inputs may be any that keep to these rules, and one draw needn't show every extreme that they name: `segments`: each row is one worker's block; ids never fall along a row, every segment has 1 to 128 slots and one has exactly 128. `routes`: within the 256 tokens of one worker no expert is named more than 40 times, a bound that some block reaches. `page_table`: each row lists every page of one worker's pool once; its first 16 entries take the worker's blocks in order.
All inputs are finite; a program needn't handle non-finite values.
Results may differ from a plain program's by a relative error of at most 0.019.
Values may be sent and summed in bfloat16 or wider, within the bound.
A program may use at most 192 MiB of HBM per device.

v0:
```python
import jax
import jax.numpy as jnp
from jax import lax
from jax.sharding import PartitionSpec as P

HEAD = 128
PAGE = 16


norm_eps = 1e-05
rope_base = 500000.0


def partner(block, axis, distance):
    count = lax.axis_size(axis)
    route = []
    for low in range(count):
        high = low | 1 << distance
        if high != low and high < count:
            route += [(low, high), (high, low)]
    return lax.ppermute(block, axis, route)


def rms_scale(inputs, gain_vec):
    return (
        inputs * lax.rsqrt(jnp.mean(inputs * inputs, axis=-1, keepdims=True) + norm_eps) * gain_vec
    )


def in_segment(segment_row):
    row_count = segment_row.shape[0]
    row_order = jnp.arange(row_count, dtype=jnp.int32)
    earlier = jnp.concatenate([segment_row[:1] - 1, segment_row[:-1]])
    starts = jnp.where(segment_row != earlier, row_order, 0)
    return row_order - lax.cummax(starts, axis=0)


def rotate(inputs, position):
    half_size = inputs.shape[-1] // 2
    inv_freq = rope_base ** (-jnp.arange(half_size, dtype=jnp.float32) * 2.0 / inputs.shape[-1])
    angles = position.astype(jnp.float32)[:, None] * inv_freq[None, :]
    cosine = jnp.cos(angles)[:, None, :]
    sine_term = jnp.sin(angles)[:, None, :]
    leading = inputs[..., :half_size]
    trailing = inputs[..., half_size:]
    return jnp.concatenate(
        [leading * cosine - trailing * sine_term, trailing * cosine + leading * sine_term], axis=-1
    )


def shards(
    tokens,
    segments,
    routes,
    page_table,
    cache_pool,
    attn_gain,
    w_query,
    w_keyval,
    w_out,
    ffn_gain,
    w_router,
    expert_gate,
    expert_up,
    expert_down,
    shared_gate,
    shared_up,
    shared_down,
):
    tp_count = lax.axis_size("tp")
    seq_count = lax.axis_size("seq")
    tp_rank = lax.axis_index("tp")
    row_count = tokens.shape[0]
    col_width = tokens.shape[1]
    model_width = col_width * tp_count
    whole_rows = lax.all_gather(tokens, "tp", axis=1, tiled=True)
    residual = whole_rows.astype(jnp.float32)
    normed_in = rms_scale(residual, attn_gain).astype(jnp.bfloat16)
    segment_row = segments[0]
    position = in_segment(segment_row)
    local_heads = w_query.shape[1] // HEAD
    queries = jnp.dot(normed_in, w_query, preferred_element_type=jnp.float32).reshape(
        row_count, local_heads, HEAD
    )
    queries = rotate(queries, position).astype(jnp.bfloat16)
    keyval = jnp.dot(normed_in, w_keyval, preferred_element_type=jnp.float32)
    if w_keyval.shape[1] == HEAD:
        is_key = tp_rank % 2 == 0
        rotated = rotate(keyval.reshape(row_count, 1, HEAD), position).reshape(row_count, HEAD)
        own_half = jnp.where(is_key, rotated, keyval).astype(jnp.bfloat16)
        other_half = partner(own_half, "tp", 0)
        key_rows = jnp.where(is_key, own_half, other_half)
        values = jnp.where(is_key, other_half, own_half)
        cache_rows = own_half
    else:
        key_rows = (
            rotate(keyval[:, :HEAD].reshape(row_count, 1, HEAD), position)
            .reshape(row_count, HEAD)
            .astype(jnp.bfloat16)
        )
        values = keyval[:, HEAD:].astype(jnp.bfloat16)
        cache_rows = jnp.concatenate([key_rows, values], axis=1)
    scores = jnp.einsum(
        "qhd,kd->hqk", queries, key_rows, preferred_element_type=jnp.float32
    ) * HEAD ** (-0.5)
    row_order = jnp.arange(row_count, dtype=jnp.int32)
    allowed = (segment_row[:, None] == segment_row[None, :]) & (
        row_order[None, :] <= row_order[:, None]
    )
    weights = jnp.where(allowed[None], jnp.exp(scores), 0.0)
    attn_probs = (weights / jnp.sum(weights, axis=-1, keepdims=True)).astype(jnp.bfloat16)
    attended = jnp.einsum("hqk,kd->qhd", attn_probs, values, preferred_element_type=jnp.float32)
    attended = attended.astype(jnp.bfloat16).reshape(row_count, local_heads * HEAD)
    attn_part = jnp.dot(attended, w_out, preferred_element_type=jnp.float32)
    column_start = tp_rank * col_width
    attn_whole = lax.psum(attn_part.astype(jnp.bfloat16), "tp").astype(jnp.float32)
    hidden_state = residual + attn_whole
    normed_mid = rms_scale(hidden_state, ffn_gain).astype(jnp.bfloat16)
    hidden_mine = lax.dynamic_slice_in_dim(hidden_state, column_start, col_width, 1)
    logits = jnp.dot(normed_mid, w_router, preferred_element_type=jnp.float32)
    lifted = jnp.exp(jnp.take_along_axis(logits, routes, axis=1))
    route_weight = lifted / jnp.sum(lifted, axis=1, keepdims=True)
    shared_gate_out = jnp.einsum(
        "td,fd->tf", normed_mid, shared_gate, preferred_element_type=jnp.float32
    )
    shared_up_out = jnp.einsum(
        "td,fd->tf", normed_mid, shared_up, preferred_element_type=jnp.float32
    )
    shared_act = (jax.nn.silu(shared_gate_out) * shared_up_out).astype(jnp.bfloat16)
    shared_part = jnp.dot(shared_act, shared_down, preferred_element_type=jnp.float32)
    top_count = routes.shape[1]
    local_experts = expert_gate.shape[0]
    expert_total = local_experts * seq_count
    capacity = (
        (row_count * top_count * 5 // (expert_total * 3) + tp_count - 1) // tp_count * tp_count
    )
    flat_routes = routes.reshape(-1)
    onehot = (flat_routes[:, None] == jnp.arange(expert_total, dtype=jnp.int32)[None, :]).astype(
        jnp.int32
    )
    slot_rank = jnp.sum((jnp.cumsum(onehot, axis=0) - onehot) * onehot, axis=1)
    slot_index = flat_routes * capacity + slot_rank
    token_ids = jnp.arange(row_count * top_count, dtype=jnp.int32) // top_count
    outgoing = (
        jnp.zeros((expert_total * capacity, model_width), jnp.bfloat16)
        .at[slot_index]
        .set(normed_mid[token_ids])
    )
    outgoing = outgoing.reshape(seq_count, local_experts, capacity, model_width)
    slot_rows = lax.all_to_all(outgoing, "seq", split_axis=0, concat_axis=0, tiled=True)
    gate_out = jnp.einsum(
        "secd,efd->secf", slot_rows, expert_gate, preferred_element_type=jnp.float32
    )
    up_out = jnp.einsum("secd,efd->secf", slot_rows, expert_up, preferred_element_type=jnp.float32)
    activation = (jax.nn.silu(gate_out) * up_out).astype(jnp.bfloat16)
    group_part = jnp.einsum(
        "secf,efd->secd", activation, expert_down, preferred_element_type=jnp.float32
    ).astype(jnp.bfloat16)
    returned = lax.all_to_all(group_part, "seq", split_axis=0, concat_axis=0, tiled=True)
    picked = returned.reshape(expert_total * capacity, model_width)[slot_index].reshape(
        row_count, top_count, model_width
    )
    routed_part = jnp.sum(route_weight[:, :, None] * picked.astype(jnp.float32), axis=1)
    summand = shared_part + routed_part
    output_share = lax.psum_scatter(
        summand.astype(jnp.bfloat16), "tp", scatter_dimension=1, tiled=True
    ).astype(jnp.float32)
    layer_out = (hidden_mine + output_share).astype(jnp.bfloat16)
    page_count = row_count // PAGE
    new_pages = cache_rows.reshape(page_count, PAGE, cache_rows.shape[1])
    cache_out = cache_pool.at[page_table[0, :page_count]].set(new_pages)
    return (layer_out, cache_out)


def solution(mesh):
    in_specs = (
        P("seq", "tp"),
        P("seq", None),
        P("seq", None),
        P("seq", None),
        P("seq", None, "tp"),
        P(),
        P(None, "tp"),
        P(None, "tp"),
        P("tp", None),
        P(),
        P(),
        P("seq", "tp", None),
        P("seq", "tp", None),
        P("seq", "tp", None),
        P("tp", None),
        P("tp", None),
        P("tp", None),
    )
    out_specs = (P("seq", "tp"), P("seq", None, "tp"))
    return jax.shard_map(shards, mesh=mesh, in_specs=in_specs, out_specs=out_specs, check_vma=False)
```

profile of v0, /device:TPU:0, one launch (start us, length us, event | category | flops | bytes accessed | tf_op | source)
XLA Modules:
  0.0 855.5 jit_solution(13315507696775119481)
XLA Ops:
  7.2 0.7 all-gather.2.cloned.1.call-update
  8.0 1.2 slice.48
  9.8 0.8 compare_select_fusion.4
  10.6 0.3 reduce-window.15
  11.1 0.8 copy.68
  12.2 1.5 fusion.50
  13.7 0.5 multiply_cosine_fusion
  14.3 0.8 fusion.34
  15.1 15.4 %all-gather.2.cloned.1.call-done = bf16[256,2560]{1,0:T(8,128)(2,1)} async-done(((bf16[256,640]{1,0:T(8,128)(2,1)}), bf16[256,2560]{1,0:T(8,128)(2,1)}) %all-gather.2.cloned.1.call-update) | async-done | bytes 1310736 | tf_op jit(solution)/shard_map/all_gather | solution.py:76
  30.5 1.7 fusion.18
  32.2 3.9 fusion.43
  36.0 1.2 reshape.362
  37.3 0.3 fusion.72
  37.6 2.5 fusion.45
  40.2 0.3 fusion.57
  40.7 0.4 copy-done.9
  41.1 1.4 fusion.27
  42.6 1.9 convolution_convert_fusion.1
  44.5 2.0 convolution_convert_fusion
  46.7 18.1 %reduce-window.19 = s32[64,12,128]{2,1,0:T(8,128)S(1)} reduce-window(s32[64,12,128]{2,1,0:T(8,128)S(1)} %copy-done.5, s32[]{:T(128)} %constant.37.clone.1), window={size=1x1x128 pad=0_0x0_0x127_0}, to_apply=%region_7.8 | reduce-window | flops 12484608 | bytes 786436 | tf_op jit(solution)/shard_map/reduce-window.2
  64.8 0.2 slice.71
  65.0 0.3 copy.70
  65.8 0.2 broadcast_add_fusion
  66.0 0.2 fusion.37
  66.2 19.4 %all-reduce.2.cloned.1.call-done = bf16[256,2560]{1,0:T(8,128)(2,1)} async-done(((bf16[256,2560]{1,0:T(8,128)(2,1)}), bf16[256,2560]{1,0:T(8,128)(2,1)}) %all-reduce.2.cloned.1.call-update) | async-done | bytes 1310736 | tf_op jit(solution)/shard_map/psum | solution.py:116
  85.7 3.3 convert_add_fusion
  89.0 0.5 multiply_convert_fusion
  89.6 43.1 %scatter_custom_fusion = bf16[2560,2560]{1,0:T(8,128)(2,1)} fusion(s32[1536]{0:T(1024)S(1)} %fusion.63, bf16[256,2560]{1,0:T(8,128)(2,1)S(1)} %multiply_convert_fusion, s32[2048]{0:T(1024)S(1)} %pad_clamp_fusion.1, bf16[]{:T(256)} %constant.74.clone.1), kind=kCustom, calls=%fused_computation.15 | custom fusion | bytes 13107202 | tf_op jit(solution)/shard_map/scatter | solution.py:147
  132.6 291.2 %all_to_all.10 = bf16[8,8,40,2560]{3,2,1,0:T(8,128)(2,1)} all-to-all(bf16[8,8,40,2560]{3,2,1,0:T(8,128)(2,1)} %bitcast.119), channel_id=1, replica_groups=mesh['seq'=8,'tp'=4] {'seq'}, dimensions={0} | all-to-all | bytes 26214400 | tf_op jit(solution)/shard_map/all_to_all | solution.py:150
  423.9 14.2 %fusion.2 = f32[8,8,40,384]{3,2,1,0:T(8,128)} fusion(bf16[8,384,2560]{2,1,0:T(8,128)(2,1)} %param.29, bf16[8,8,40,2560]{3,2,1,0:T(8,128)(2,1)} %all_to_all.10), kind=kOutput, calls=%fused_computation.8 | convolution fusion | flops 5033164800 | bytes 32768000 | tf_op jit(solution)/shard_map/secd,efd->secf/dot_general | solution.py:154
  438.0 24.0 %convert_bitcast_fusion = bf16[8,8,40,2560]{3,2,0,1:T(8,128)(2,1)} fusion(bf16[8,384,2560]{2,1,0:T(8,128)(2,1)} %param.30, f32[8,8,40,384]{3,2,1,0:T(8,128)} %fusion.2, bf16[8,384,2560]{2,1,0:T(8,128)(2,1)} %param.28, bf16[8,8,40,2560]{3,2,1,0:T(8,128)(2,1)} %all_to_all.10), kind=kOutput, calls=%fused_computation.12 | convolution fusion | flops 10078781440 | bytes 61603840 | tf_op jit(solution)/shard_map/secf,efd->secd/dot_general | solution.py:156
  462.0 12.3 %copy.74 = bf16[8,8,40,2560]{3,2,1,0:T(8,128)(2,1)} copy(bf16[8,8,40,2560]{3,2,0,1:T(8,128)(2,1)} %convert_bitcast_fusion) | data formatting | bytes 26214400 | tf_op jit(solution)/shard_map/convert_element_type | solution.py:158
  474.4 5.5 all-to-all-start.1
  479.9 0.3 reduce-scatter.4.cloned.1.call-start
  480.6 0.5 fusion.75
  481.1 12.7 %gather_fusion.1 = f32[1536]{0:T(1024)S(1)} fusion(f32[256,64]{0,1:T(8,128)S(1)} %fusion.75, s32[1536]{0:T(1024)S(1)} %reshape.386), kind=kCustom, calls=%fused_computation.2 | custom fusion | bytes 24576 | tf_op jit(solution)/shard_map/jit(take_along_axis)/gather | solution.py:121
  494.2 2.4 fusion.74
  496.6 266.6 %all-to-all-done.1 = bf16[8,8,40,2560]{3,2,1,0:T(8,128)(2,1)} async-done(((bf16[8,8,40,2560]{3,2,1,0:T(8,128)(2,1)}), bf16[8,8,40,2560]{3,2,1,0:T(8,128)(2,1)}, u32[]{:S(2)}, u32[]{:S(2)}) %all-to-all-start.1) | async-done | bytes 13107232 | tf_op jit(solution)/shard_map/all_to_all | solution.py:159
  763.2 21.5 %gather_fusion = bf16[1536,2560]{1,0:T(8,128)(2,1)} fusion(bf16[2560,2560]{1,0:T(8,128)(2,1)} %bitcast.26, s32[2048]{0:T(1024)S(1)} %pad_clamp_fusion), kind=kCustom, calls=%fused_computation.1 | custom fusion | bytes 15734784 | tf_op jit(solution)/shard_map/gather | solution.py:160
  784.7 14.2 %reshape.369 = f32[256,6,2560]{2,1,0:T(8,128)} reshape(bf16[1536,2560]{1,0:T(8,128)(2,1)} %gather_fusion) | data formatting | bytes 23592960 | tf_op jit(solution)/shard_map/convert_element_type | solution.py:163
  798.9 12.8 %multiply_reduce_fusion = f32[256,2560]{1,0:T(8,128)} fusion(f32[256,6,2560]{2,1,0:T(8,128)} %reshape.369, f32[256,6]{1,0:T(8,128)S(1)} %copy.66), kind=kLoop, calls=%fused_computation.5 | loop fusion | flops 7208960 | bytes 18356224 | tf_op jit(solution)/shard_map/reduce_sum | solution.py:163
  811.8 5.6 fusion.17
  817.4 2.6 copy.82
  820.1 0.9 slice.83
  821.1 1.0 scatter_fusion
  822.2 23.3 %reduce-scatter.4.cloned.1.call-done = bf16[640,256]{1,0:T(8,128)(2,1)} async-done(((bf16[2560,256]{1,0:T(8,128)(2,1)}), bf16[640,256]{1,0:T(8,128)(2,1)}) %reduce-scatter.4.cloned.1.call-update) | async-done | bytes 327696
  845.5 1.2 copy.83
  846.7 1.9 add_convert_fusion
  (73 shorter events, 2.3 us)
Async XLA Ops:
  7.2 37.3 %copy-start = (bf16[512,2560]{1,0:T(8,128)(2,1)S(1)}, bf16[512,2560]{1,0:T(8,128)(2,1)}, u32[]{:S(2)}) copy-start(bf16[512,2560]{1,0:T(8,128)(2,1)} %param.25) | copy-start | bytes 7864324
  7.2 25.0 %copy-start.17 = (f32[2560]{0:T(1024)S(1)}, f32[2560]{0:T(1024)}, u32[]{:S(2)}) copy-start(f32[2560]{0:T(1024)} %param.22) | copy-start | bytes 30724
  7.2 23.3 %all-gather.2.cloned.1.call-start = ((), (), s32[]{:S(2)}) async-start(), calls=%async_computation.3 | async-start | bytes 1638400 | tf_op jit(solution)/shard_map/all_gather | solution.py:76
  7.9 77.7 %all-reduce.2.cloned.1.call-start = ((), (), s32[]{:S(2)}) async-start(), calls=%async_computation.4 | async-start | bytes 2621440 | tf_op jit(solution)/shard_map/psum | solution.py:116
  37.6 3.5 copy-start.13
  40.1 4.3 copy-start.15
  40.5 0.6 copy-start.9
  40.5 0.6 copy-start.11
  44.5 2.0 copy-start.14
  44.5 2.2 copy-start.5
  46.5 39.2 %copy-start.2 = (bf16[256,2560]{1,0:T(8,128)(2,1)S(1)}, bf16[256,2560]{1,0:T(8,128)(2,1)}, u32[]{:S(2)}) copy-start(bf16[256,2560]{1,0:T(8,128)(2,1)} %all-gather.2.cloned.1.call-done) | copy-start | bytes 3932164
  66.2 22.8 %copy-start.16 = (f32[2560]{0:T(1024)S(1)}, f32[2560]{0:T(1024)}, u32[]{:S(2)}) copy-start(f32[2560]{0:T(1024)} %param.26) | copy-start | bytes 30724
  85.7 3.4 copy-start.3
  85.7 3.4 copy-start.4
  474.4 6.2 copy-start.8
  474.4 288.8 %all-to-all-start.1 = ((bf16[8,8,40,2560]{3,2,1,0:T(8,128)(2,1)}), bf16[8,8,40,2560]{3,2,1,0:T(8,128)(2,1)}, u32[]{:S(2)}, u32[]{:S(2)}) async-start(bf16[8,8,40,2560]{3,2,1,0:T(8,128)(2,1)} %copy.74), calls=%async_computation.1 | async-start | bytes 26214400 | tf_op jit(solution)/shard_map/all_to_all | solution.py:159
  479.9 365.6 %reduce-scatter.4.cloned.1.call-start = ((), (), s32[]{:S(2)}) async-start(), calls=%async_computation.5 | async-start | bytes 1638400
  817.4 2.6 copy-start.18
  817.4 3.6 copy-start.10
  817.4 3.6 copy-start.12
  817.4 3.7 copy-start.7
  817.4 31.2 %copy-start.1 = (bf16[512,2560]{1,0:T(8,128)(2,1)S(1)}, bf16[512,2560]{1,0:T(8,128)(2,1)}, u32[]{:S(2)}) copy-start(bf16[512,2560]{1,0:T(8,128)(2,1)} %param.25) | copy-start | bytes 7864324
  822.2 26.4 %copy-start.6 = (bf16[32,16,256]{2,1,0:T(8,128)(2,1)}, bf16[32,16,256]{2,1,0:T(8,128)(2,1)S(1)}, u32[]{:S(2)}) copy-start(bf16[32,16,256]{2,1,0:T(8,128)(2,1)S(1)} %scatter_fusion) | copy-start | bytes 786436
Sparse Core Ops, SparseCore 0:
  9.6 20.8 all-gather.1
  46.6 38.9 all-reduce.1
  820.1 25.3 reduce-scatter.3
where the time goes:
time: 864 us; the launch traced here: 856 us
  waiting for transfers between devices  325 us (38%)
  blocking collectives  291 us (34%)
  local copies, waits for them, and re-layouts  116 us (13%)
  matrix products  58.4 us (7%)
  other arithmetic  43.6 us (5%)
  between operations  15.3 us (2%)
    all_to_all x1, blocking collectives, shards(): lax.all_to_all(outgoing, 'seq', split_axis=0, concat_axis=0, tiled=True)  291 us
    all_to_all x1, waiting for transfers between devices, shards(): lax.all_to_all(group_part, 'seq', split_axis=0, concat_axis=0, tiled=True)  267 us
    scatter x1, local copies, waits for them, and re-layouts, shards(): outgoing = jnp.zeros((expert_total * capacity, model_width), jnp.bfloat16...  43.1 us
    unnamed x4, waiting for transfers between devices  24 us
    dot_general x1, matrix products, shards(): jnp.einsum('secf,efd->secd', activation, expert_down, preferred_element_t...  24 us
    gather x1, local copies, waits for them, and re-layouts, shards(): returned.reshape(expert_total * capacity, model_width)[slot_index]  21.5 us
    psum x1, waiting for transfers between devices, shards(): lax.psum(attn_part.astype(jnp.bfloat16), 'tp').astype(jnp.float32)  19.4 us
    another operation x7, other arithmetic  19.2 us
  transfers between devices with their start and end apart: 4, of which 4 were waited for; matrix products, arithmetic and copies ran while one was open for 5% of the time, Pallas kernels for 0%

commit v1 on v0

--- a/solution.py
+++ b/solution.py
@@ -21,6 +21,15 @@
     return lax.ppermute(block, axis, route)
 
 
+def gather_all(block):
+    return lax.all_gather(block, ("seq", "tp"), axis=0)
+
+
+def scatter_all(whole):
+    part = lax.psum_scatter(whole, "tp", scatter_dimension=2, tiled=True)
+    return lax.psum_scatter(part, "seq", scatter_dimension=0, tiled=False)
+
+
 def rms_scale(inputs, gain_vec):
     return (
         inputs * lax.rsqrt(jnp.mean(inputs * inputs, axis=-1, keepdims=True) + norm_eps) * gain_vec
@@ -28,11 +37,11 @@
 
 
 def in_segment(segment_row):
-    row_count = segment_row.shape[0]
-    row_order = jnp.arange(row_count, dtype=jnp.int32)
-    earlier = jnp.concatenate([segment_row[:1] - 1, segment_row[:-1]])
-    starts = jnp.where(segment_row != earlier, row_order, 0)
-    return row_order - lax.cummax(starts, axis=0)
+    row_order = jnp.arange(segment_row.shape[0], dtype=jnp.int32)
+    before = (segment_row[:, None] == segment_row[None, :]) & (
+        row_order[None, :] < row_order[:, None]
+    )
+    return jnp.sum(before.astype(jnp.int32), axis=1)
 
 
 def rotate(inputs, position):
@@ -112,59 +121,77 @@
     attended = jnp.einsum("hqk,kd->qhd", attn_probs, values, preferred_element_type=jnp.float32)
     attended = attended.astype(jnp.bfloat16).reshape(row_count, local_heads * HEAD)
     attn_part = jnp.dot(attended, w_out, preferred_element_type=jnp.float32)
-    column_start = tp_rank * col_width
-    attn_whole = lax.psum(attn_part.astype(jnp.bfloat16), "tp").astype(jnp.float32)
-    hidden_state = residual + attn_whole
-    normed_mid = rms_scale(hidden_state, ffn_gain).astype(jnp.bfloat16)
-    hidden_mine = lax.dynamic_slice_in_dim(hidden_state, column_start, col_width, 1)
-    logits = jnp.dot(normed_mid, w_router, preferred_element_type=jnp.float32)
-    lifted = jnp.exp(jnp.take_along_axis(logits, routes, axis=1))
-    route_weight = lifted / jnp.sum(lifted, axis=1, keepdims=True)
-    shared_gate_out = jnp.einsum(
-        "td,fd->tf", normed_mid, shared_gate, preferred_element_type=jnp.float32
-    )
-    shared_up_out = jnp.einsum(
-        "td,fd->tf", normed_mid, shared_up, preferred_element_type=jnp.float32
-    )
-    shared_act = (jax.nn.silu(shared_gate_out) * shared_up_out).astype(jnp.bfloat16)
-    shared_part = jnp.dot(shared_act, shared_down, preferred_element_type=jnp.float32)
+    attn_mine = lax.psum_scatter(
+        attn_part.astype(jnp.bfloat16), "tp", scatter_dimension=1, tiled=True
+    )
+    hidden_mine = tokens.astype(jnp.float32) + attn_mine.astype(jnp.float32)
+    seq_rank = lax.axis_index("seq")
+    gathered = gather_all(hidden_mine.astype(jnp.bfloat16))
+    hidden_all = (
+        gathered.reshape(seq_count, tp_count, row_count, col_width)
+        .transpose(0, 2, 1, 3)
+        .reshape(seq_count, row_count, model_width)
+    )
+    normed_all = rms_scale(hidden_all.astype(jnp.float32), ffn_gain).astype(jnp.bfloat16)
+
     top_count = routes.shape[1]
     local_experts = expert_gate.shape[0]
     expert_total = local_experts * seq_count
     capacity = (
         (row_count * top_count * 5 // (expert_total * 3) + tp_count - 1) // tp_count * tp_count
     )
-    flat_routes = routes.reshape(-1)
-    onehot = (flat_routes[:, None] == jnp.arange(expert_total, dtype=jnp.int32)[None, :]).astype(
-        jnp.int32
-    )
-    slot_rank = jnp.sum((jnp.cumsum(onehot, axis=0) - onehot) * onehot, axis=1)
-    slot_index = flat_routes * capacity + slot_rank
-    token_ids = jnp.arange(row_count * top_count, dtype=jnp.int32) // top_count
-    outgoing = (
-        jnp.zeros((expert_total * capacity, model_width), jnp.bfloat16)
-        .at[slot_index]
-        .set(normed_mid[token_ids])
-    )
-    outgoing = outgoing.reshape(seq_count, local_experts, capacity, model_width)
-    slot_rows = lax.all_to_all(outgoing, "seq", split_axis=0, concat_axis=0, tiled=True)
+    slots = local_experts * capacity
+    routes_all = lax.all_gather(routes, "seq", axis=0)
+    chosen = jnp.sum(
+        (routes_all[:, :, :, None] == jnp.arange(expert_total, dtype=jnp.int32)).astype(
+            jnp.float32
+        ),
+        axis=2,
+    )
+    logits = jnp.einsum("wtd,de->wte", normed_all, w_router, preferred_element_type=jnp.float32)
+    lifted = jnp.where(chosen > 0, jnp.exp(logits), 0.0)
+    route_weight = lifted / jnp.sum(lifted, axis=2, keepdims=True)
+    first = seq_rank * local_experts
+    named = lax.dynamic_slice_in_dim(chosen, first, local_experts, 2)
+    weight_mine = lax.dynamic_slice_in_dim(route_weight, first, local_experts, 2)
+    earlier = (row_order[:, None] > row_order[None, :]).astype(jnp.bfloat16)
+    rank = jnp.einsum(
+        "ts,wse->wte", earlier, named.astype(jnp.bfloat16), preferred_element_type=jnp.float32
+    ).astype(jnp.int32)
+    place = jnp.where(named > 0, rank, -1)
+    hit = place.transpose(0, 2, 1)[:, :, None, :] == jnp.arange(capacity, dtype=jnp.int32)[
+        None, None, :, None
+    ]
+    select = hit.astype(jnp.bfloat16).reshape(seq_count, slots, row_count)
+    slot_weight = jnp.sum(
+        jnp.where(hit, weight_mine.transpose(0, 2, 1)[:, :, None, :], 0.0), axis=3
+    )
+    slot_rows = jnp.einsum(
+        "wst,wtd->wsd", select, normed_all, preferred_element_type=jnp.float32
+    ).astype(jnp.bfloat16).reshape(seq_count, local_experts, capacity, model_width)
     gate_out = jnp.einsum(
         "secd,efd->secf", slot_rows, expert_gate, preferred_element_type=jnp.float32
     )
     up_out = jnp.einsum("secd,efd->secf", slot_rows, expert_up, preferred_element_type=jnp.float32)
-    activation = (jax.nn.silu(gate_out) * up_out).astype(jnp.bfloat16)
+    activation = (jax.nn.silu(gate_out) * up_out * slot_weight[..., None]).astype(jnp.bfloat16)
     group_part = jnp.einsum(
         "secf,efd->secd", activation, expert_down, preferred_element_type=jnp.float32
-    ).astype(jnp.bfloat16)
-    returned = lax.all_to_all(group_part, "seq", split_axis=0, concat_axis=0, tiled=True)
-    picked = returned.reshape(expert_total * capacity, model_width)[slot_index].reshape(
-        row_count, top_count, model_width
-    )
-    routed_part = jnp.sum(route_weight[:, :, None] * picked.astype(jnp.float32), axis=1)
-    summand = shared_part + routed_part
-    output_share = lax.psum_scatter(
-        summand.astype(jnp.bfloat16), "tp", scatter_dimension=1, tiled=True
-    ).astype(jnp.float32)
+    ).astype(jnp.bfloat16).reshape(seq_count, slots, model_width)
+    normed_mid = lax.dynamic_index_in_dim(normed_all, seq_rank, 0, keepdims=False)
+    shared_gate_out = jnp.einsum(
+        "td,fd->tf", normed_mid, shared_gate, preferred_element_type=jnp.float32
+    )
+    shared_up_out = jnp.einsum(
+        "td,fd->tf", normed_mid, shared_up, preferred_element_type=jnp.float32
+    )
+    shared_act = (jax.nn.silu(shared_gate_out) * shared_up_out).astype(jnp.bfloat16)
+    shared_part = jnp.dot(shared_act, shared_down, preferred_element_type=jnp.float32)
+    routed_part = jnp.einsum(
+        "wst,wsd->wtd", select, group_part, preferred_element_type=jnp.float32
+    )
+    is_mine = jnp.arange(seq_count, dtype=jnp.int32)[:, None, None] == seq_rank
+    summand = routed_part + jnp.where(is_mine, shared_part[None], 0.0)
+    output_share = scatter_all(summand.astype(jnp.bfloat16)).astype(jnp.float32)
     layer_out = (hidden_mine + output_share).astype(jnp.bfloat16)
     page_count = row_count // PAGE
     new_pages = cache_rows.reshape(page_count, PAGE, cache_rows.shape[1])

time: 864 us -> 481 us (0.56)
  blocking collectives: 291 us -> 30.6 us
  waiting for transfers between devices: 325 us -> 253 us
  local copies, waits for them, and re-layouts: 116 us -> 72.8 us
  matrix products: 58.4 us -> 84.5 us
  other arithmetic: 43.6 us -> 24.3 us
    all_to_all x1 -> x0, blocking collectives: 291 us -> none  [shards(): lax.all_to_all(outgoing, 'seq', split_axis=0, concat_axis=0, tiled=True)]
    all_to_all x1 -> x0, waiting for transfers between devices: 267 us -> none  [shards(): lax.all_to_all(group_part, 'seq', split_axis=0, concat_axis=0, tiled=True)]
    unnamed x4 -> x7, waiting for transfers between devices: 24 us -> 111 us
    reduce_scatter x0 -> x1, waiting for transfers between devices: none -> 64.7 us  [scatter_all(): return lax.psum_scatter(part, 'seq', scatter_dimension=0, tiled=False)]
    all_gather x0 -> x1, waiting for transfers between devices: none -> 56.6 us  [gather_all(): return lax.all_gather(block, ('seq', 'tp'), axis=0)]
    scatter x1 -> x0, local copies, waits for them, and re-layouts: 43.1 us -> none  [shards(): outgoing = jnp.zeros((expert_total * capacity, model_width), jnp.bfloat16...]
    unnamed x41 -> x38, local copies, waits for them, and re-layouts: 5.13 us -> 40.6 us
    gather x6 -> x0, local copies, waits for them, and re-layouts: 34.7 us -> none  [the longest x1 21.5 us: shards(): returned.reshape(expert_total * capacity, model_width)[slot_index]]
  transfers between devices with their start and end apart: 4 -> 5, of which waited for: 4 -> 5; matrix products, arithmetic and copies ran while one was open for 5% -> 2% of each run, Pallas kernels for 0% -> 0%
where the time goes in v1:
time: 481 us; the launch traced here: 479 us
  waiting for transfers between devices  253 us (53%)
  matrix products  84.5 us (18%)
  local copies, waits for them, and re-layouts  72.8 us (15%)
  blocking collectives  30.6 us (6%)
  other arithmetic  24.3 us (5%)
  between operations  14.1 us (3%)
    unnamed x7, waiting for transfers between devices  111 us
    reduce_scatter x1, waiting for transfers between devices, scatter_all(): return lax.psum_scatter(part, 'seq', scatter_dimension=0, tiled=False)  64.7 us
    all_gather x1, waiting for transfers between devices, gather_all(): return lax.all_gather(block, ('seq', 'tp'), axis=0)  56.6 us
    unnamed x38, local copies, waits for them, and re-layouts  40.6 us
    all_gather x1, blocking collectives, shards(): routes_all = lax.all_gather(routes, 'seq', axis=0)  30.6 us
    dot_general x1, matrix products, shards(): jnp.einsum('secf,efd->secd', activation, expert_down, preferred_element_t...  24 us
    all_gather x1, waiting for transfers between devices, shards(): whole_rows = lax.all_gather(tokens, 'tp', axis=1, tiled=True)  20.2 us
    dot_general x1, matrix products, shards(): jnp.einsum('secd,efd->secf', slot_rows, expert_up, preferred_element_type...  14.1 us
  transfers between devices with their start and end apart: 5, of which 5 were waited for; matrix products, arithmetic and copies ran while one was open for 2% of the time, Pallas kernels for 0%

profile of v1, /device:TPU:0, one launch (start us, length us, event | category | flops | bytes accessed | tf_op | source)
XLA Modules:
  0.0 479.4 jit_solution(7024119431726332237)
XLA Ops:
  7.2 0.7 all-gather.5.cloned.1.call-update
  8.0 0.9 convert_reduce_fusion.1
  8.9 0.9 compare_and_fusion.1
  9.7 0.5 multiply_cosine_fusion
  10.3 20.2 %all-gather.5.cloned.1.call-done = bf16[256,2560]{1,0:T(8,128)(2,1)} async-done(((bf16[256,640]{1,0:T(8,128)(2,1)}), bf16[256,2560]{1,0:T(8,128)(2,1)}) %all-gather.5.cloned.1.call-update) | async-done | bytes 1310736 | tf_op jit(solution)/shard_map/all_gather | solution.py:85
  30.5 1.7 fusion.15
  32.2 3.9 fusion.56
  36.0 1.2 reshape.242
  37.2 2.5 fusion.58
  39.8 0.3 fusion.72
  40.1 0.3 fusion.88
  40.7 1.4 fusion.24
  42.1 1.9 convolution_convert_fusion.2
  44.1 2.0 convolution_convert_fusion.1
  46.0 2.4 copy.76
  48.5 26.6 %reduce-scatter.10.cloned.1.call-done = bf16[640,256]{1,0:T(8,128)(2,1)} async-done(((bf16[2560,256]{1,0:T(8,128)(2,1)}), bf16[640,256]{1,0:T(8,128)(2,1)}) %reduce-scatter.10.cloned.1.call-update) | async-done | bytes 327696
  75.2 1.2 copy.77
  76.4 0.8 fusion.49
  77.3 30.6 %all-gather = s32[2048,6]{0,1:T(8,128)S(1)} all-gather(s32[256,6]{0,1:T(8,128)S(1)} %copy-done.13), channel_id=2, replica_groups=mesh['seq'=8,'tp'=4] {'seq'}, dimensions={0}, use_global_device_ids=true | all-gather | bytes 55296 | tf_op jit(solution)/shard_map/all_gather | solution.py:144
  108.0 0.4 convert_reduce_fusion
  108.4 0.2 fusion.47
  108.6 0.4 bitcast_compare_fusion
  109.1 56.6 %all-gather.7.cloned.1.call-done = bf16[8192,640]{1,0:T(8,128)(2,1)} async-done(((bf16[256,640]{1,0:T(8,128)(2,1)}), bf16[8192,640]{1,0:T(8,128)(2,1)}) %all-gather.7.cloned.1.call-update) | async-done | bytes 10485776 | tf_op jit(solution)/shard_map/all_gather | solution.py:25
  165.7 6.1 %multiply_reduce_fusion = f32[8192]{0:T(1024)S(1)} fusion(bf16[8192,640]{1,0:T(8,128)(2,1)} %all-gather.7.cloned.1.call-done), kind=kLoop, calls=%fused_computation.1 | loop fusion | flops 15720448 | bytes 10518528 | tf_op jit(solution)/shard_map/reduce_sum | solution.py:35
  171.9 13.8 %copy.83 = f32[8,4,32,8,640]{4,3,1,2,0:T(8,128)} copy(bf16[8,4,32,8,640]{4,3,2,1,0:T(8,128)(2,1)} %bitcast.139) | data formatting | bytes 31457280 | tf_op jit(solution)/shard_map/convert_element_type | solution.py:135
  185.7 8.4 %multiply_convert_fusion = bf16[8,256,2560]{2,1,0:T(8,128)(2,1)S(1)} fusion(f32[8,256,2560]{2,1,0:T(8,128)} %bitcast.136, f32[2560]{0:T(1024)S(1)} %copy-done.12, f32[8,256]{1,0:T(8,128)S(1)} %add_rsqrt_fusion), kind=kLoop, calls=%fused_computation.3 | loop fusion | flops 15728640 | bytes 31475712 | tf_op jit(solution)/shard_map/convert_element_type | solution.py:135
  194.1 3.3 fusion.89
  197.3 0.6 copy-done.2
  198.0 0.5 select_reduce_fusion
  198.5 10.5 %convolution_convert_fusion = bf16[8,320,2560]{2,1,0:T(8,128)(2,1)} fusion(pred[8,320,256]{2,1,0:T(32,128)(4,1)S(1)} %bitcast_compare_fusion, bf16[8,256,2560]{2,1,0:T(8,128)(2,1)} %copy-done.2), kind=kOutput, calls=%fused_computation.13 | convolution fusion | flops 3361996800 | bytes 24248320 | tf_op jit(solution)/shard_map/wst,wtd->wsd/dot_general | solution.py:169
  209.1 14.1 %fusion.2 = f32[8,8,40,384]{3,2,1,0:T(8,128)} fusion(bf16[8,384,2560]{2,1,0:T(8,128)(2,1)} %param.29, bf16[8,8,40,2560]{3,2,1,0:T(8,128)(2,1)} %bitcast.140), kind=kOutput, calls=%fused_computation.6 | convolution fusion | flops 5033164800 | bytes 32768000 | tf_op jit(solution)/shard_map/secd,efd->secf/dot_general | solution.py:175
  223.1 24.0 %convert_bitcast_fusion = bf16[8,8,40,2560]{3,2,0,1:T(8,128)(2,1)} fusion(bf16[8,384,2560]{2,1,0:T(8,128)(2,1)} %param.30, f32[8,8,40,384]{3,2,1,0:T(8,128)} %fusion.2, bf16[8,384,2560]{2,1,0:T(8,128)(2,1)} %param.28, bf16[8,8,40,2560]{3,2,1,0:T(8,128)(2,1)} %bitcast.141, f32[8,8,40]{2,0,1:T(8,128)S(1)} %copy.67), kind=kOutput, calls=%fused_computation.10 | convolution fusion | flops 10079764480 | bytes 61614080 | tf_op jit(solution)/shard_map/secf,efd->secd/dot_general | solution.py:177
  247.2 12.5 %copy.68 = bf16[8,8,40,2560]{3,2,1,0:T(8,128)(2,1)} copy(bf16[8,8,40,2560]{3,2,0,1:T(8,128)(2,1)} %convert_bitcast_fusion) | data formatting | bytes 26214400 | tf_op jit(solution)/shard_map/convert_element_type | solution.py:179
  259.6 2.9 fusion.31
  262.6 4.3 fusion.43
  266.9 13.5 %add_convert_fusion = bf16[8,256,2560]{2,1,0:T(8,128)(2,1)} fusion(f32[256,2560]{1,0:T(8,128)S(1)} %fusion.43, pred[8]{0:T(512)(128)(4,1)S(1)} %iota_compare_fusion.5, pred[8,320,256]{2,1,0:T(32,128)(4,1)} %copy-done.4, bf16[8,320,2560]{2,1,0:T(8,128)(2,1)} %bitcast.142), kind=kOutput, calls=%fused_computation.2 | convolution fusion | flops 3371171840 | bytes 26869768 | tf_op jit(solution)/shard_map/wst,wsd->wtd/dot_general | solution.py:189
  280.4 14.7 %copy.78 = bf16[8,256,2560]{1,0,2:T(8,128)(2,1)} copy(bf16[8,256,2560]{2,1,0:T(8,128)(2,1)} %add_convert_fusion) | data formatting | bytes 20971520
  295.0 12.4 %copy.84 = bf16[320,8,8,256]{3,1,2,0:T(8,128)(2,1)} copy(bf16[320,8,8,256]{3,2,1,0:T(8,128)(2,1)} %bitcast.138) | data formatting | bytes 20971520
  307.5 83.9 %reduce-scatter.12.cloned.1.call-done = bf16[640,2048]{1,0:T(8,128)(2,1)} async-done(((bf16[2560,2048]{1,0:T(8,128)(2,1)}), bf16[640,2048]{1,0:T(8,128)(2,1)}) %reduce-scatter.12.cloned.1.call-update) | async-done | bytes 2621456
  391.4 4.1 copy.85
  395.6 5.0 %copy.79 = bf16[8,256,640]{2,1,0:T(8,128)(2,1)} copy(bf16[8,256,640]{1,0,2:T(8,128)(2,1)} %bitcast.143) | data formatting | bytes 5242880
  400.6 0.9 slice.42
  401.5 0.8 fusion.78
  402.3 0.7 pad_maximum_fusion
  403.0 1.7 copy.69
  404.6 1.7 scatter_fusion
  406.4 64.7 %reduce-scatter.8.cloned.1.call-done = bf16[1,256,640]{2,1,0:T(8,128)(2,1)} async-done(((bf16[8,256,640]{2,1,0:T(8,128)(2,1)}), bf16[1,256,640]{2,1,0:T(8,128)(2,1)}) %reduce-scatter.8.cloned.1.call-update) | async-done | bytes 327696 | tf_op jit(solution)/shard_map/reduce_scatter | solution.py:30
  471.1 1.8 fusion.48
  (54 shorter events, 0.8 us)
Async XLA Ops:
  7.2 36.9 %copy-start = (bf16[512,2560]{1,0:T(8,128)(2,1)S(1)}, bf16[512,2560]{1,0:T(8,128)(2,1)}, u32[]{:S(2)}) copy-start(bf16[512,2560]{1,0:T(8,128)(2,1)} %param.25) | copy-start | bytes 7864324
  7.2 23.3 %all-gather.5.cloned.1.call-start = ((), (), s32[]{:S(2)}) async-start(), calls=%async_computation.3 | async-start | bytes 1638400 | tf_op jit(solution)/shard_map/all_gather | solution.py:85
  7.9 67.3 %reduce-scatter.10.cloned.1.call-start = ((), (), s32[]{:S(2)}) async-start(), calls=%async_computation.6 | async-start | bytes 1638400
  10.3 27.0 %copy-start.14 = (f32[2560]{0:T(1024)S(1)}, f32[2560]{0:T(1024)}, u32[]{:S(2)}) copy-start(f32[2560]{0:T(1024)} %param.22) | copy-start | bytes 30724
  39.7 0.9 copy-start.11
  40.1 0.6 copy-start.9
  40.1 0.6 copy-start.10
  44.1 32.3 %copy-start.3 = (bf16[256,640]{1,0:T(8,128)(2,1)S(1)}, bf16[256,640]{1,0:T(8,128)(2,1)}, u32[]{:S(2)}) copy-start(bf16[256,640]{1,0:T(8,128)(2,1)} %param.17) | copy-start | bytes 983044
  46.0 31.3 %copy-start.13 = (s32[256,6]{0,1:T(8,128)S(1)}, s32[256,6]{0,1:T(8,128)}, u32[]{:S(2)}) copy-start(s32[256,6]{0,1:T(8,128)} %param.19) | copy-start | bytes 18436
  48.5 117.2 %all-gather.7.cloned.1.call-start = ((), (), s32[]{:S(2)}) async-start(), calls=%async_computation.5 | async-start | bytes 10813440 | tf_op jit(solution)/shard_map/all_gather | solution.py:25
  77.2 314.3 %reduce-scatter.12.cloned.1.call-start = ((), (), s32[]{:S(2)}) async-start(), calls=%async_computation.7 | async-start | bytes 13107200
  109.0 89.5 %copy-start.4 = (pred[8,320,256]{2,1,0:T(32,128)(4,1)}, pred[8,320,256]{2,1,0:T(32,128)(4,1)S(1)}, u32[]{:S(2)}) copy-start(pred[8,320,256]{2,1,0:T(32,128)(4,1)S(1)} %bitcast_compare_fusion) | copy-start | bytes 1966084
  171.9 13.8 %copy-start.12 = (f32[2560]{0:T(1024)S(1)}, f32[2560]{0:T(1024)}, u32[]{:S(2)}) copy-start(f32[2560]{0:T(1024)} %param.26) | copy-start | bytes 30724
  185.6 8.4 %copy-start.8 = (bf16[2560,64]{0,1:T(8,128)(2,1)S(1)}, bf16[2560,64]{0,1:T(8,128)(2,1)}, u32[]{:S(2)}) copy-start(bf16[2560,64]{0,1:T(8,128)(2,1)} %param.27) | copy-start | bytes 983044
  194.0 3.9 copy-start.2
  247.2 12.5 %copy-start.5 = (bf16[384,2560]{1,0:T(8,128)(2,1)S(1)}, bf16[384,2560]{1,0:T(8,128)(2,1)}, u32[]{:S(2)}) copy-start(bf16[384,2560]{1,0:T(8,128)(2,1)} %param.31) | copy-start | bytes 5898244
  307.5 163.6 %reduce-scatter.8.cloned.1.call-start = ((), (), s32[]{:S(2)}) async-start(), calls=%async_computation.4 | async-start | bytes 2949120 | tf_op jit(solution)/shard_map/reduce_scatter | solution.py:30
  395.6 77.3 %copy-start.1 = (bf16[512,2560]{1,0:T(8,128)(2,1)S(1)}, bf16[512,2560]{1,0:T(8,128)(2,1)}, u32[]{:S(2)}) copy-start(bf16[512,2560]{1,0:T(8,128)(2,1)} %param.25) | copy-start | bytes 7864324
  395.6 5.0 %copy-start.15 = (s32[1,32]{1,0:T(1,128)S(1)}, s32[1,32]{1,0:T(1,128)}, u32[]{:S(2)}) copy-start(s32[1,32]{1,0:T(1,128)} %param.20) | copy-start | bytes 388
  395.6 9.1 %copy-start.7 = (bf16[32,16,256]{2,1,0:T(8,128)(2,1)S(1)}, bf16[32,16,256]{2,1,0:T(8,128)(2,1)}, u32[]{:S(2)}) copy-start(bf16[32,16,256]{2,1,0:T(8,128)(2,1)} %param.21) | copy-start | bytes 786436
  406.3 66.6 %copy-start.6 = (bf16[32,16,256]{2,1,0:T(8,128)(2,1)}, bf16[32,16,256]{2,1,0:T(8,128)(2,1)S(1)}, u32[]{:S(2)}) copy-start(bf16[32,16,256]{2,1,0:T(8,128)(2,1)S(1)} %scatter_fusion) | copy-start | bytes 786436
Sparse Core Ops, SparseCore 0:
  9.6 20.8 all-gather.4
  48.6 26.5 reduce-scatter.9
  79.0 86.6 all-gather.6
  307.6 83.8 reduce-scatter.11
  400.7 70.3 reduce-scatter.7

commit v2 on v1

--- a/solution.py
+++ b/solution.py
@@ -1,6 +1,8 @@
 import jax
 import jax.numpy as jnp
 from jax import lax
+from jax.experimental import pallas as pl
+from jax.experimental.pallas import tpu as pltpu
 from jax.sharding import PartitionSpec as P
 
 HEAD = 128
@@ -26,8 +28,86 @@
 
 
 def scatter_all(whole):
-    part = lax.psum_scatter(whole, "tp", scatter_dimension=2, tiled=True)
+    part = lax.psum_scatter(whole, "tp", scatter_dimension=0, tiled=False)
     return lax.psum_scatter(part, "seq", scatter_dimension=0, tiled=False)
+
+
+def dispatch_body(rows_ref, select_ref, gain_ref, router_ref, slot_ref, logit_ref):
+    parts, _, width = rows_ref.shape
+    total = None
+    for part in range(parts):
+        block = rows_ref[part].astype(jnp.float32)
+        square = jnp.sum(block * block, axis=1, keepdims=True)
+        total = square if total is None else total + square
+    scale = lax.rsqrt(total / (parts * width) + norm_eps)
+    select = select_ref[...]
+    logit = None
+    for part in range(parts):
+        columns = slice(part * width, (part + 1) * width)
+        normed = (
+            rows_ref[part].astype(jnp.float32) * scale * gain_ref[:, columns]
+        ).astype(jnp.bfloat16)
+        slot_ref[:, columns] = jnp.dot(
+            select, normed, preferred_element_type=jnp.float32
+        ).astype(jnp.bfloat16)
+        term = jnp.dot(normed, router_ref[columns, :], preferred_element_type=jnp.float32)
+        logit = term if logit is None else logit + term
+    logit_ref[...] = logit
+
+
+def dispatch(gathered, select, gain, router):
+    workers, parts, rows, width = gathered.shape
+    slots = select.shape[1]
+    model_width = parts * width
+    return pl.pallas_call(
+        dispatch_body,
+        grid=(workers,),
+        in_specs=[
+            pl.BlockSpec((None, parts, rows, width), lambda w: (w, 0, 0, 0)),
+            pl.BlockSpec((None, slots, rows), lambda w: (w, 0, 0)),
+            pl.BlockSpec((1, model_width), lambda w: (0, 0)),
+            pl.BlockSpec((model_width, router.shape[1]), lambda w: (0, 0)),
+        ],
+        out_specs=[
+            pl.BlockSpec((None, slots, model_width), lambda w: (w, 0, 0)),
+            pl.BlockSpec((None, rows, router.shape[1]), lambda w: (w, 0, 0)),
+        ],
+        out_shape=[
+            jax.ShapeDtypeStruct((workers, slots, model_width), jnp.bfloat16),
+            jax.ShapeDtypeStruct((workers, rows, router.shape[1]), jnp.float32),
+        ],
+        compiler_params=pltpu.CompilerParams(vmem_limit_bytes=32 << 20),
+    )(gathered, select, gain[None, :], router)
+
+
+def combine_body(parts, place_ref, expert_ref, shared_ref, out_ref):
+    width = out_ref.shape[2]
+    place = place_ref[...]
+    is_mine = pl.program_id(0) == lax.axis_index("seq")
+    for part in range(parts):
+        columns = slice(part * width, (part + 1) * width)
+        routed = jnp.dot(place, expert_ref[:, columns], preferred_element_type=jnp.float32)
+        out_ref[part] = (routed + jnp.where(is_mine, shared_ref[:, columns], 0.0)).astype(
+            jnp.bfloat16
+        )
+
+
+def combine(place, expert_rows, shared_part, parts):
+    workers, rows, slots = place.shape
+    model_width = expert_rows.shape[2]
+    width = model_width // parts
+    return pl.pallas_call(
+        lambda *refs: combine_body(parts, *refs),
+        grid=(workers,),
+        in_specs=[
+            pl.BlockSpec((None, rows, slots), lambda w: (w, 0, 0)),
+            pl.BlockSpec((None, slots, model_width), lambda w: (w, 0, 0)),
+            pl.BlockSpec((rows, model_width), lambda w: (0, 0)),
+        ],
+        out_specs=pl.BlockSpec((parts, None, rows, width), lambda w: (0, w, 0, 0)),
+        out_shape=jax.ShapeDtypeStruct((parts, workers, rows, width), jnp.bfloat16),
+        compiler_params=pltpu.CompilerParams(vmem_limit_bytes=32 << 20),
+    )(place, expert_rows, shared_part)
 
 
 def rms_scale(inputs, gain_vec):
@@ -122,17 +202,17 @@
     attended = attended.astype(jnp.bfloat16).reshape(row_count, local_heads * HEAD)
     attn_part = jnp.dot(attended, w_out, preferred_element_type=jnp.float32)
     attn_mine = lax.psum_scatter(
-        attn_part.astype(jnp.bfloat16), "tp", scatter_dimension=1, tiled=True
+        attn_part.astype(jnp.bfloat16)
+        .reshape(row_count, tp_count, col_width)
+        .transpose(1, 0, 2),
+        "tp",
+        scatter_dimension=0,
+        tiled=False,
     )
     hidden_mine = tokens.astype(jnp.float32) + attn_mine.astype(jnp.float32)
     seq_rank = lax.axis_index("seq")
     gathered = gather_all(hidden_mine.astype(jnp.bfloat16))
-    hidden_all = (
-        gathered.reshape(seq_count, tp_count, row_count, col_width)
-        .transpose(0, 2, 1, 3)
-        .reshape(seq_count, row_count, model_width)
-    )
-    normed_all = rms_scale(hidden_all.astype(jnp.float32), ffn_gain).astype(jnp.bfloat16)
+    gathered = gathered.reshape(seq_count, tp_count, row_count, col_width)
 
     top_count = routes.shape[1]
     local_experts = expert_gate.shape[0]
@@ -140,20 +220,16 @@
     capacity = (
         (row_count * top_count * 5 // (expert_total * 3) + tp_count - 1) // tp_count * tp_count
     )
+    capacity = (capacity + 15) // 16 * 16
     slots = local_experts * capacity
-    routes_all = lax.all_gather(routes, "seq", axis=0)
-    chosen = jnp.sum(
-        (routes_all[:, :, :, None] == jnp.arange(expert_total, dtype=jnp.int32)).astype(
-            jnp.float32
-        ),
-        axis=2,
-    )
-    logits = jnp.einsum("wtd,de->wte", normed_all, w_router, preferred_element_type=jnp.float32)
-    lifted = jnp.where(chosen > 0, jnp.exp(logits), 0.0)
-    route_weight = lifted / jnp.sum(lifted, axis=2, keepdims=True)
+    marks = jnp.sum(
+        (routes[:, :, None] == jnp.arange(expert_total, dtype=jnp.int32)).astype(jnp.float32),
+        axis=1,
+    ).astype(jnp.bfloat16)
+    marks = jnp.pad(marks, ((0, 0), (0, -expert_total % 128)))
+    chosen = lax.all_gather(marks, "seq", axis=0)[:, :, :expert_total].astype(jnp.float32)
     first = seq_rank * local_experts
     named = lax.dynamic_slice_in_dim(chosen, first, local_experts, 2)
-    weight_mine = lax.dynamic_slice_in_dim(route_weight, first, local_experts, 2)
     earlier = (row_order[:, None] > row_order[None, :]).astype(jnp.bfloat16)
     rank = jnp.einsum(
         "ts,wse->wte", earlier, named.astype(jnp.bfloat16), preferred_element_type=jnp.float32
@@ -163,12 +239,17 @@
         None, None, :, None
     ]
     select = hit.astype(jnp.bfloat16).reshape(seq_count, slots, row_count)
+    place_back = (
+        place[:, :, :, None] == jnp.arange(capacity, dtype=jnp.int32)[None, None, None, :]
+    ).astype(jnp.bfloat16).reshape(seq_count, row_count, slots)
+    slot_rows, logits = dispatch(gathered, select, ffn_gain, w_router)
+    slot_rows = slot_rows.reshape(seq_count, local_experts, capacity, model_width)
+    lifted = jnp.where(chosen > 0, jnp.exp(logits), 0.0)
+    route_weight = lifted / jnp.sum(lifted, axis=2, keepdims=True)
+    weight_mine = lax.dynamic_slice_in_dim(route_weight, first, local_experts, 2)
     slot_weight = jnp.sum(
         jnp.where(hit, weight_mine.transpose(0, 2, 1)[:, :, None, :], 0.0), axis=3
     )
-    slot_rows = jnp.einsum(
-        "wst,wtd->wsd", select, normed_all, preferred_element_type=jnp.float32
-    ).astype(jnp.bfloat16).reshape(seq_count, local_experts, capacity, model_width)
     gate_out = jnp.einsum(
         "secd,efd->secf", slot_rows, expert_gate, preferred_element_type=jnp.float32
     )
@@ -177,7 +258,9 @@
     group_part = jnp.einsum(
         "secf,efd->secd", activation, expert_down, preferred_element_type=jnp.float32
     ).astype(jnp.bfloat16).reshape(seq_count, slots, model_width)
-    normed_mid = lax.dynamic_index_in_dim(normed_all, seq_rank, 0, keepdims=False)
+    own_rows = lax.dynamic_index_in_dim(gathered, seq_rank, 0, keepdims=False)
+    own_rows = own_rows.transpose(1, 0, 2).reshape(row_count, model_width)
+    normed_mid = rms_scale(own_rows.astype(jnp.float32), ffn_gain).astype(jnp.bfloat16)
     shared_gate_out = jnp.einsum(
         "td,fd->tf", normed_mid, shared_gate, preferred_element_type=jnp.float32
     )
@@ -186,12 +269,8 @@
     )
     shared_act = (jax.nn.silu(shared_gate_out) * shared_up_out).astype(jnp.bfloat16)
     shared_part = jnp.dot(shared_act, shared_down, preferred_element_type=jnp.float32)
-    routed_part = jnp.einsum(
-        "wst,wsd->wtd", select, group_part, preferred_element_type=jnp.float32
-    )
-    is_mine = jnp.arange(seq_count, dtype=jnp.int32)[:, None, None] == seq_rank
-    summand = routed_part + jnp.where(is_mine, shared_part[None], 0.0)
-    output_share = scatter_all(summand.astype(jnp.bfloat16)).astype(jnp.float32)
+    summand = combine(place_back, group_part, shared_part, tp_count)
+    output_share = scatter_all(summand).astype(jnp.float32)
     layer_out = (hidden_mine + output_share).astype(jnp.bfloat16)
     page_count = row_count // PAGE
     new_pages = cache_rows.reshape(page_count, PAGE, cache_rows.shape[1])

time: 481 us -> 442 us (0.919)
  local copies, waits for them, and re-layouts: 72.8 us -> 47.6 us
  Pallas kernels: 0 us -> 24.6 us
  matrix products: 84.5 us -> 60 us
  waiting for transfers between devices: 253 us -> 242 us
    unnamed x7 -> x5, waiting for transfers between devices: 111 us -> 0.08 us
    reduce_scatter x0 -> x2, waiting for transfers between devices: none -> 111 us  [the longest x1 83.9 us: scatter_all(): part = lax.psum_scatter(whole, 'tp', scatter_dimension=0, tiled=False)]
    dot_general x3 -> x0, matrix products: 27.3 us -> none  [the longest x1 13.5 us: shards(): jnp.einsum('wst,wsd->wtd', select, group_part, preferred_element_type=jnp...]
    unnamed x38 -> x32, local copies, waits for them, and re-layouts: 40.6 us -> 14 us
    pallas_call x0 -> x2, Pallas kernels: none -> 24.6 us  [the longest x1 12.9 us: dispatch(): pl.pallas_call(dispatch_body, grid=(workers,), in_specs=[pl.BlockSpec((No...]
    all_gather x1, waiting for transfers between devices: 56.6 us -> 42.5 us  [gather_all(): return lax.all_gather(block, ('seq', 'tp'), axis=0)]
    convert_element_type x1 -> x3, local copies, waits for them, and re-layouts: 13.8 us -> 6.16 us  [the longest x1 3.25 us: shards(): own_rows.astype(jnp.float32)]
    eq x2 -> x4, local copies, waits for them, and re-layouts: 0.08 us -> 5.6 us  [shards(): place[:, :, :, None]]
  transfers between devices with their start and end apart: 5 -> 5, of which waited for: 5 -> 5; matrix products, arithmetic and copies ran while one was open for 2% -> 5% of each run, Pallas kernels for 0% -> 0%
where the time goes in v2:
time: 442 us; the launch traced here: 441 us
  waiting for transfers between devices  242 us (55%)
  matrix products  60 us (14%)
  local copies, waits for them, and re-layouts  47.6 us (11%)
  blocking collectives  32 us (7%)
  Pallas kernels  24.6 us (6%)
  other arithmetic  20.8 us (5%)
  between operations  14.1 us (3%)
    reduce_scatter x1, waiting for transfers between devices, scatter_all(): part = lax.psum_scatter(whole, 'tp', scatter_dimension=0, tiled=False)  83.9 us
    reduce_scatter x1, waiting for transfers between devices, scatter_all(): return lax.psum_scatter(part, 'seq', scatter_dimension=0, tiled=False)  69.5 us
    all_gather x1, waiting for transfers between devices, gather_all(): return lax.all_gather(block, ('seq', 'tp'), axis=0)  42.5 us
    all_gather x1, blocking collectives, shards(): lax.all_gather(marks, 'seq', axis=0)[:, :, :expert_total]  32 us
    dot_general x1, matrix products, shards(): jnp.einsum('secf,efd->secd', activation, expert_down, preferred_element_t...  27.2 us
    reduce_scatter x1, waiting for transfers between devices, shards(): lax.psum_scatter(attn_part.astype(jnp.bfloat16).reshape(row_count, tp_cou...  26.6 us
    all_gather x1, waiting for transfers between devices, shards(): whole_rows = lax.all_gather(tokens, 'tp', axis=1, tiled=True)  19.1 us
    dot_general x1, matrix products, shards(): jnp.einsum('secd,efd->secf', slot_rows, expert_up, preferred_element_type...  15.6 us
  transfers between devices with their start and end apart: 5, of which 5 were waited for; matrix products, arithmetic and copies ran while one was open for 5% of the time, Pallas kernels for 0%

profile of v2, /device:TPU:0, one launch (start us, length us, event | category | flops | bytes accessed | tf_op | source)
XLA Modules:
  0.0 441.0 jit_solution(15679268962872008743)
XLA Ops:
  7.2 1.8 copy.133
  9.1 0.9 convert_reduce_fusion.1
  10.0 0.9 compare_and_fusion.1
  10.9 0.5 multiply_cosine_fusion
  11.4 19.1 %all-gather.5.cloned.1.call-done = bf16[256,2560]{1,0:T(8,128)(2,1)} async-done(((bf16[256,640]{1,0:T(8,128)(2,1)}), bf16[256,2560]{1,0:T(8,128)(2,1)}) %all-gather.5.cloned.1.call-update) | async-done | bytes 1310736 | tf_op jit(solution)/shard_map/all_gather | solution.py:165
  30.5 1.7 fusion.24
  32.2 3.9 fusion.46
  36.0 1.2 reshape.246
  37.6 2.5 fusion.48
  40.6 1.4 fusion.34
  42.0 1.9 convolution_convert_fusion.1
  43.9 1.9 convolution_convert_fusion
  45.9 1.6 copy.94
  47.5 1.4 copy.95
  49.0 26.6 %reduce-scatter.4.cloned.1.call-done = bf16[1,256,640]{2,1,0:T(8,128)(2,1)} async-done(((bf16[4,256,640]{2,1,0:T(8,128)(2,1)}), bf16[1,256,640]{2,1,0:T(8,128)(2,1)}) %reduce-scatter.4.cloned.1.call-update) | async-done | bytes 327696 | tf_op jit(solution)/shard_map/reduce_scatter | solution.py:204
  75.6 1.8 fusion.39
  77.6 32.0 %all-gather = bf16[2048,128]{0,1:T(8,128)(2,1)S(1)} all-gather(bf16[256,128]{0,1:T(8,128)(2,1)S(1)} %pad.4), channel_id=2, replica_groups=mesh['seq'=8,'tp'=4] {'seq'}, dimensions={0}, use_global_device_ids=true | all-gather | bytes 589824 | tf_op jit(solution)/shard_map/all_gather | solution.py:230
  110.0 0.6 convolution_convert_fusion.2
  110.5 1.3 copy.98
  111.9 1.6 bitcast_select_fusion
  114.1 1.3 copy.102.router_ref
  115.5 1.9 eq.90
  117.3 3.6 copy.100
  121.3 3.4 compare_convert_fusion.refs_0_
  124.7 42.5 %all-gather.7.cloned.1.call-done = bf16[8192,640]{1,0:T(8,128)(2,1)} async-done(((bf16[256,640]{1,0:T(8,128)(2,1)}), bf16[8192,640]{1,0:T(8,128)(2,1)}) %all-gather.7.cloned.1.call-update) | async-done | bytes 10485776 | tf_op jit(solution)/shard_map/all_gather | solution.py:27
  167.2 3.0 convert_bitcast_fusion.1
  170.2 1.7 fusion.27
  171.9 3.2 copy.108
  175.1 4.0 copy-done.3
  179.1 12.9 %shard_map.176 = (bf16[8,384,2560]{2,1,0:T(8,128)(2,1)}, f32[8,256,64]{2,1,0:T(8,128)S(1)}) custom-call(bf16[8,4,256,640]{3,2,1,0:T(8,128)(2,1)S(1)} %bitcast.119, bf16[8,384,256]{2,1,0:T(8,128)(2,1)S(1)} %fusion.15.select_ref, f32[1,2560]{1,0:T(1,128)S(1)} %broadcast_in_dim.30.gain_ref, bf16[2560,64]{1,0:T(8,128)(2,1)S(1)} %copy.102.router_ref), custom_call_target="tpu_custom_call" | custom-call | tf_op jit(solution)/shard_map/pallas_call | solution.py:62
  192.4 0.6 fusion.37
  193.3 0.7 select_reduce_fusion
  194.0 15.6 %fusion.2 = f32[8,8,48,384]{3,2,1,0:T(8,128)} fusion(bf16[8,384,2560]{2,1,0:T(8,128)(2,1)} %param.29, bf16[8,8,48,2560]{3,2,1,0:T(8,128)(2,1)} %bitcast.132), kind=kOutput, calls=%fused_computation.3 | convolution fusion | flops 6039797760 | bytes 36175872 | tf_op jit(solution)/shard_map/secd,efd->secf/dot_general | solution.py:256
  209.6 27.2 %convert_bitcast_fusion = bf16[8,8,48,2560]{3,2,0,1:T(8,128)(2,1)} fusion(bf16[8,384,2560]{2,1,0:T(8,128)(2,1)} %param.30, f32[8,8,48,384]{3,2,1,0:T(8,128)} %fusion.2, bf16[8,384,2560]{2,1,0:T(8,128)(2,1)} %param.28, bf16[8,8,48,2560]{3,2,1,0:T(8,128)(2,1)} %bitcast.133, f32[8,8,48]{2,0,1:T(8,128)S(1)} %copy.106), kind=kOutput, calls=%fused_computation.7 | convolution fusion | flops 12095717376 | bytes 67645440 | tf_op jit(solution)/shard_map/secf,efd->secd/dot_general | solution.py:258
  236.8 13.5 %copy.107 = bf16[8,8,48,2560]{3,2,1,0:T(8,128)(2,1)} copy(bf16[8,8,48,2560]{3,2,0,1:T(8,128)(2,1)} %convert_bitcast_fusion) | data formatting | bytes 31457280 | tf_op jit(solution)/shard_map/convert_element_type | solution.py:260
  250.7 1.0 copy-done.5
  252.2 0.9 fusion.76
  253.1 4.2 fusion.36.refs_2_
  257.3 1.4 copy-done.4
  258.7 11.6 %shard_map.177 = bf16[4,8,256,640]{3,2,1,0:T(8,128)(2,1)S(1)} custom-call(bf16[8,256,384]{2,1,0:T(8,128)(2,1)S(1)} %copy-done.4, bf16[8,384,2560]{2,1,0:T(8,128)(2,1)} %bitcast.120, f32[256,2560]{1,0:T(8,128)S(1)} %fusion.36.refs_2_), custom_call_target="tpu_custom_call" | custom-call | tf_op jit(solution)/shard_map/pallas_call | solution.py:99
  270.3 4.0 copy-done.2
  274.4 83.9 %reduce-scatter.6.cloned.1.call-done = bf16[1,8,256,640]{3,2,1,0:T(8,128)(2,1)} async-done(((bf16[4,8,256,640]{3,2,1,0:T(8,128)(2,1)}), bf16[1,8,256,640]{3,2,1,0:T(8,128)(2,1)}) %reduce-scatter.6.cloned.1.call-update) | async-done | bytes 2621456 | tf_op jit(solution)/shard_map/reduce_scatter | solution.py:31
  358.3 0.9 slice.50
  359.2 0.7 pad_maximum_fusion
  359.9 1.0 copy.109
  360.9 2.2 scatter_fusion
  363.1 69.5 %reduce-scatter.8.cloned.1.call-done = bf16[1,256,640]{2,1,0:T(8,128)(2,1)} async-done(((bf16[8,256,640]{2,1,0:T(8,128)(2,1)}), bf16[1,256,640]{2,1,0:T(8,128)(2,1)}) %reduce-scatter.8.cloned.1.call-update) | async-done | bytes 327696 | tf_op jit(solution)/shard_map/reduce_scatter | solution.py:32
  432.6 1.8 fusion.38
  (60 shorter events, 4.1 us)
Async XLA Ops:
  7.2 36.8 %copy-start = (bf16[512,2560]{1,0:T(8,128)(2,1)S(1)}, bf16[512,2560]{1,0:T(8,128)(2,1)}, u32[]{:S(2)}) copy-start(bf16[512,2560]{1,0:T(8,128)(2,1)} %param.25) | copy-start | bytes 7864324
  7.2 23.3 %all-gather.5.cloned.1.call-start = ((), (), s32[]{:S(2)}) async-start(), calls=%async_computation.3 | async-start | bytes 1638400 | tf_op jit(solution)/shard_map/all_gather | solution.py:165
  9.1 66.6 %reduce-scatter.4.cloned.1.call-start = ((), (), s32[]{:S(2)}) async-start(), calls=%async_computation.4 | async-start | bytes 1638400 | tf_op jit(solution)/shard_map/reduce_scatter | solution.py:204
  36.0 1.6 copy-start.13
  40.1 3.8 copy-start.10
  47.5 28.2 %copy-start.7 = (bf16[256,640]{1,0:T(8,128)(2,1)S(1)}, bf16[256,640]{1,0:T(8,128)(2,1)}, u32[]{:S(2)}) copy-start(bf16[256,640]{1,0:T(8,128)(2,1)} %param.17) | copy-start | bytes 983044
  47.5 30.0 %copy-start.12 = (s32[256,6]{0,1:T(8,128)S(1)}, s32[256,6]{0,1:T(8,128)}, u32[]{:S(2)}) copy-start(s32[256,6]{0,1:T(8,128)} %param.19) | copy-start | bytes 18436
  49.0 118.3 %all-gather.7.cloned.1.call-start = ((), (), s32[]{:S(2)}) async-start(), calls=%async_computation.7 | async-start | bytes 10813440 | tf_op jit(solution)/shard_map/all_gather | solution.py:27
  77.4 280.8 %reduce-scatter.6.cloned.1.call-start = ((), (), s32[]{:S(2)}) async-start(), calls=%async_computation.5 | async-start | bytes 13107200 | tf_op jit(solution)/shard_map/reduce_scatter | solution.py:31
  111.9 3.6 copy-start.11
  175.1 4.0 copy-start.3
  236.8 13.5 %copy-start.6 = (f32[256,4,640]{0,2,1:T(8,128)S(1)}, f32[256,4,640]{0,2,1:T(8,128)}, u32[]{:S(2)}) copy-start(f32[256,4,640]{0,2,1:T(8,128)} %copy.108) | copy-start | bytes 7864324
  250.2 1.9 copy-start.8
  250.7 1.1 copy-start.5
  257.3 1.4 copy-start.4
  270.3 4.0 copy-start.2
  274.3 84.0 %copy-start.14 = (s32[1,32]{1,0:T(1,128)S(1)}, s32[1,32]{1,0:T(1,128)}, u32[]{:S(2)}) copy-start(s32[1,32]{1,0:T(1,128)} %param.20) | copy-start | bytes 388
  274.3 158.3 %copy-start.9 = (bf16[1,256,640]{2,1,0:T(8,128)(2,1)S(1)}, bf16[1,256,640]{2,1,0:T(8,128)(2,1)}, u32[]{:S(2)}) copy-start(bf16[1,256,640]{2,1,0:T(8,128)(2,1)} %reduce-scatter.4.cloned.1.call-done) | copy-start | bytes 983044
  274.3 160.1 %copy-start.1 = (bf16[512,2560]{1,0:T(8,128)(2,1)S(1)}, bf16[512,2560]{1,0:T(8,128)(2,1)}, u32[]{:S(2)}) copy-start(bf16[512,2560]{1,0:T(8,128)(2,1)} %param.25) | copy-start | bytes 7864324
  274.3 158.3 %reduce-scatter.8.cloned.1.call-start = ((), (), s32[]{:S(2)}) async-start(), calls=%async_computation.6 | async-start | bytes 2949120 | tf_op jit(solution)/shard_map/reduce_scatter | solution.py:32
Sparse Core Ops, SparseCore 0:
  9.6 20.8 all-gather.4
  49.1 26.5 reduce-scatter.3
  79.4 87.7 all-gather.6
  274.4 83.8 reduce-scatter.5
  362.0 70.5 reduce-scatter.7

commit v3 on v2

--- a/solution.py
+++ b/solution.py
@@ -227,7 +227,13 @@
         axis=1,
     ).astype(jnp.bfloat16)
     marks = jnp.pad(marks, ((0, 0), (0, -expert_total % 128)))
-    chosen = lax.all_gather(marks, "seq", axis=0)[:, :, :expert_total].astype(jnp.float32)
+    shifted = [marks]
+    for shift in range(1, seq_count):
+        shifted.append(
+            lax.ppermute(marks, "seq", [(i, (i + shift) % seq_count) for i in range(seq_count)])
+        )
+    turn = (seq_rank - jnp.arange(seq_count, dtype=jnp.int32)) % seq_count
+    chosen = jnp.stack(shifted)[turn][:, :, :expert_total].astype(jnp.float32)
     first = seq_rank * local_experts
     named = lax.dynamic_slice_in_dim(chosen, first, local_experts, 2)
     earlier = (row_order[:, None] > row_order[None, :]).astype(jnp.bfloat16)

time: 442 us -> 442 us (level)
  blocking collectives: 32 us -> 0 us
  waiting for transfers between devices: 242 us -> 260 us
  starting transfers between devices: 0.21 us -> 12.4 us
    all_gather x1 -> x0, blocking collectives: 32 us -> none  [shards(): lax.all_gather(marks, 'seq', axis=0)[:, :, :expert_total]]
    all_gather x1, waiting for transfers between devices: 42.5 us -> 56.6 us  [gather_all(): return lax.all_gather(block, ('seq', 'tp'), axis=0)]
    ppermute x0 -> x7, starting transfers between devices: none -> 12.2 us  [shards(): lax.ppermute(marks, 'seq', [(i, (i + shift) % seq_count) for i in range(s...]
    ppermute x0 -> x7, waiting for transfers between devices: none -> 4.81 us  [shards(): lax.ppermute(marks, 'seq', [(i, (i + shift) % seq_count) for i in range(s...]
    unnamed x32 -> x43, local copies, waits for them, and re-layouts: 14 us -> 13.6 us
  transfers between devices with their start and end apart: 5 -> 12, of which waited for: 5 -> 8; matrix products, arithmetic and copies ran while one was open for 5% -> 5% of each run, Pallas kernels for 0% -> 0%
where the time goes in v3:
time: 442 us; the launch traced here: 441 us
  waiting for transfers between devices  260 us (59%)
  matrix products  60 us (14%)
  local copies, waits for them, and re-layouts  47.8 us (11%)
  Pallas kernels  24.6 us (6%)
  other arithmetic  21.3 us (5%)
  between operations  14.2 us (3%)
  starting transfers between devices  12.4 us (3%)
    reduce_scatter x1, waiting for transfers between devices, scatter_all(): part = lax.psum_scatter(whole, 'tp', scatter_dimension=0, tiled=False)  83.9 us
    reduce_scatter x1, waiting for transfers between devices, scatter_all(): return lax.psum_scatter(part, 'seq', scatter_dimension=0, tiled=False)  69.3 us
    all_gather x1, waiting for transfers between devices, gather_all(): return lax.all_gather(block, ('seq', 'tp'), axis=0)  56.6 us
    dot_general x1, matrix products, shards(): jnp.einsum('secf,efd->secd', activation, expert_down, preferred_element_t...  27.1 us
    reduce_scatter x1, waiting for transfers between devices, shards(): lax.psum_scatter(attn_part.astype(jnp.bfloat16).reshape(row_count, tp_cou...  26.7 us
    all_gather x1, waiting for transfers between devices, shards(): whole_rows = lax.all_gather(tokens, 'tp', axis=1, tiled=True)  19.1 us
    dot_general x1, matrix products, shards(): jnp.einsum('secd,efd->secf', slot_rows, expert_up, preferred_element_type...  15.6 us
    unnamed x43, local copies, waits for them, and re-layouts  13.6 us
  transfers between devices with their start and end apart: 12, of which 8 were waited for; matrix products, arithmetic and copies ran while one was open for 5% of the time, Pallas kernels for 0%

profile of v3, /device:TPU:0, one launch (start us, length us, event | category | flops | bytes accessed | tf_op | source)
XLA Modules:
  0.0 440.7 jit_solution(2633911514502380001)
XLA Ops:
  7.2 1.8 copy.159
  11.4 19.1 %all-gather.4.cloned.1.call-done = bf16[256,2560]{1,0:T(8,128)(2,1)} async-done(((bf16[256,640]{1,0:T(8,128)(2,1)}), bf16[256,2560]{1,0:T(8,128)(2,1)}) %all-gather.4.cloned.1.call-update) | async-done | bytes 1310736 | tf_op jit(solution)/shard_map/all_gather | solution.py:165
  30.5 1.7 fusion.24
  32.2 3.9 fusion.46
  36.0 1.2 reshape.295
  37.6 2.5 fusion.48
  40.6 1.4 fusion.34
  42.0 1.9 convolution_convert_fusion.1
  43.9 1.9 convolution_convert_fusion
  45.9 1.6 copy.113
  47.5 1.5 copy.114
  49.0 26.7 %reduce-scatter.4.cloned.1.call-done = bf16[1,256,640]{2,1,0:T(8,128)(2,1)} async-done(((bf16[4,256,640]{2,1,0:T(8,128)(2,1)}), bf16[1,256,640]{2,1,0:T(8,128)(2,1)}) %reduce-scatter.4.cloned.1.call-update) | async-done | bytes 327696 | tf_op jit(solution)/shard_map/reduce_scatter | solution.py:204
  75.7 1.8 fusion.39
  77.6 1.5 collective-permute-start
  79.2 1.5 collective-permute-start.1
  80.6 2.4 collective-permute-start.2
  83.0 1.4 collective-permute-start.3
  84.5 2.4 collective-permute-start.4
  87.4 1.5 collective-permute-start.5
  88.9 1.5 collective-permute-start.6
  90.9 2.4 collective-permute-done.4
  93.3 1.9 collective-permute-done.5
  97.3 1.3 copy.117
  98.6 1.9 bitcast_select_fusion
  101.1 1.9 eq.92
  103.0 3.7 copy.119
  106.9 3.6 compare_convert_fusion.refs_0_
  110.5 56.6 %all-gather.6.cloned.1.call-done = bf16[8192,640]{1,0:T(8,128)(2,1)} async-done(((bf16[256,640]{1,0:T(8,128)(2,1)}), bf16[8192,640]{1,0:T(8,128)(2,1)}) %all-gather.6.cloned.1.call-update) | async-done | bytes 10485776 | tf_op jit(solution)/shard_map/all_gather | solution.py:27
  167.1 3.0 convert_bitcast_fusion.1
  170.1 1.7 fusion.27
  171.8 3.3 copy.127
  175.0 4.0 copy-done.3
  179.0 12.9 %shard_map.176 = (bf16[8,384,2560]{2,1,0:T(8,128)(2,1)}, f32[8,256,64]{2,1,0:T(8,128)S(1)}) custom-call(bf16[8,4,256,640]{3,2,1,0:T(8,128)(2,1)S(1)} %bitcast.136, bf16[8,384,256]{2,1,0:T(8,128)(2,1)S(1)} %fusion.15.select_ref, f32[1,2560]{1,0:T(1,128)S(1)} %broadcast_in_dim.29.gain_ref, bf16[2560,64]{1,0:T(8,128)(2,1)S(1)} %copy.121.router_ref), custom_call_target="tpu_custom_call" | custom-call | tf_op jit(solution)/shard_map/pallas_call | solution.py:62
  193.9 15.6 %fusion.2 = f32[8,8,48,384]{3,2,1,0:T(8,128)} fusion(bf16[8,384,2560]{2,1,0:T(8,128)(2,1)} %param.29, bf16[8,8,48,2560]{3,2,1,0:T(8,128)(2,1)} %bitcast.147), kind=kOutput, calls=%fused_computation.4 | convolution fusion | flops 6039797760 | bytes 36175872 | tf_op jit(solution)/shard_map/secd,efd->secf/dot_general | solution.py:262
  209.5 27.1 %convert_bitcast_fusion = bf16[8,8,48,2560]{3,2,0,1:T(8,128)(2,1)} fusion(bf16[8,384,2560]{2,1,0:T(8,128)(2,1)} %param.30, f32[8,8,48,384]{3,2,1,0:T(8,128)} %fusion.2, bf16[8,384,2560]{2,1,0:T(8,128)(2,1)} %param.28, bf16[8,8,48,2560]{3,2,1,0:T(8,128)(2,1)} %bitcast.148, f32[8,8,48]{2,0,1:T(8,128)S(1)} %copy.125), kind=kOutput, calls=%fused_computation.8 | convolution fusion | flops 12095717376 | bytes 67645440 | tf_op jit(solution)/shard_map/secf,efd->secd/dot_general | solution.py:264
  236.7 13.5 %copy.126 = bf16[8,8,48,2560]{3,2,1,0:T(8,128)(2,1)} copy(bf16[8,8,48,2560]{3,2,0,1:T(8,128)(2,1)} %convert_bitcast_fusion) | data formatting | bytes 31457280 | tf_op jit(solution)/shard_map/convert_element_type | solution.py:266
  250.6 1.1 copy-done.5
  252.1 0.9 fusion.78
  253.0 4.2 fusion.36.refs_2_
  257.2 1.4 copy-done.4
  258.6 11.6 %shard_map.177 = bf16[4,8,256,640]{3,2,1,0:T(8,128)(2,1)S(1)} custom-call(bf16[8,256,384]{2,1,0:T(8,128)(2,1)S(1)} %copy-done.4, bf16[8,384,2560]{2,1,0:T(8,128)(2,1)} %bitcast.137, f32[256,2560]{1,0:T(8,128)S(1)} %fusion.36.refs_2_), custom_call_target="tpu_custom_call" | custom-call | tf_op jit(solution)/shard_map/pallas_call | solution.py:99
  270.2 4.0 copy-done.2
  274.3 83.9 %reduce-scatter.6.cloned.1.call-done = bf16[1,8,256,640]{3,2,1,0:T(8,128)(2,1)} async-done(((bf16[4,8,256,640]{3,2,1,0:T(8,128)(2,1)}), bf16[1,8,256,640]{3,2,1,0:T(8,128)(2,1)}) %reduce-scatter.6.cloned.1.call-update) | async-done | bytes 2621456 | tf_op jit(solution)/shard_map/reduce_scatter | solution.py:31
  358.2 0.9 slice.52
  359.8 1.0 copy.128
  360.8 2.2 scatter_fusion
  363.1 69.3 %reduce-scatter.8.cloned.1.call-done = bf16[1,256,640]{2,1,0:T(8,128)(2,1)} async-done(((bf16[8,256,640]{2,1,0:T(8,128)(2,1)}), bf16[1,256,640]{2,1,0:T(8,128)(2,1)}) %reduce-scatter.8.cloned.1.call-update) | async-done | bytes 327696 | tf_op jit(solution)/shard_map/reduce_scatter | solution.py:32
  432.4 1.8 fusion.38
  (88 shorter events, 10.9 us)
Async XLA Ops:
  7.2 36.7 %copy-start = (bf16[512,2560]{1,0:T(8,128)(2,1)S(1)}, bf16[512,2560]{1,0:T(8,128)(2,1)}, u32[]{:S(2)}) copy-start(bf16[512,2560]{1,0:T(8,128)(2,1)} %param.25) | copy-start | bytes 7864324
  7.2 23.3 %all-gather.4.cloned.1.call-start = ((), (), s32[]{:S(2)}) async-start(), calls=%async_computation.3 | async-start | bytes 1638400 | tf_op jit(solution)/shard_map/all_gather | solution.py:165
  9.1 66.6 %reduce-scatter.4.cloned.1.call-start = ((), (), s32[]{:S(2)}) async-start(), calls=%async_computation.4 | async-start | bytes 1638400 | tf_op jit(solution)/shard_map/reduce_scatter | solution.py:204
  36.0 1.6 copy-start.15
  40.1 3.8 copy-start.12
  47.4 28.3 %copy-start.8 = (bf16[256,640]{1,0:T(8,128)(2,1)S(1)}, bf16[256,640]{1,0:T(8,128)(2,1)}, u32[]{:S(2)}) copy-start(bf16[256,640]{1,0:T(8,128)(2,1)} %param.17) | copy-start | bytes 983044
  47.5 30.1 %copy-start.14 = (s32[256,6]{0,1:T(8,128)S(1)}, s32[256,6]{0,1:T(8,128)}, u32[]{:S(2)}) copy-start(s32[256,6]{0,1:T(8,128)} %param.19) | copy-start | bytes 18436
  47.5 39.5 %copy-start.11 = (bf16[2560,64]{0,1:T(8,128)(2,1)S(1)}, bf16[2560,64]{0,1:T(8,128)(2,1)}, u32[]{:S(2)}) copy-start(bf16[2560,64]{0,1:T(8,128)(2,1)} %param.27) | copy-start | bytes 983044
  47.5 39.8 %copy-start.13 = (f32[2560]{0:T(1024)S(1)}, f32[2560]{0:T(1024)}, u32[]{:S(2)}) copy-start(f32[2560]{0:T(1024)} %param.26) | copy-start | bytes 30724
  49.0 118.1 %all-gather.6.cloned.1.call-start = ((), (), s32[]{:S(2)}) async-start(), calls=%async_computation.7 | async-start | bytes 10813440 | tf_op jit(solution)/shard_map/all_gather | solution.py:27
  77.5 280.7 %reduce-scatter.6.cloned.1.call-start = ((), (), s32[]{:S(2)}) async-start(), calls=%async_computation.5 | async-start | bytes 13107200 | tf_op jit(solution)/shard_map/reduce_scatter | solution.py:31
  77.6 9.7 %collective-permute-start = (bf16[256,128]{0,1:T(8,128)(2,1)S(1)}, bf16[256,128]{0,1:T(8,128)(2,1)S(1)}, u32[]{:S(2)}, u32[]{:S(2)}) collective-permute-start(bf16[256,128]{0,1:T(8,128)(2,1)S(1)} %pad.4), channel_id=1, source_target_pairs={{0,4},{4,8},{8,12},{12,16},{16,20},{20,24},{24,28},{28,0},{1,5},{5... | collective-permute-start | bytes 196616 | tf_op jit(solution)/shard_map/ppermute | solution.py:233
  79.2 9.7 %collective-permute-start.1 = (bf16[256,128]{0,1:T(8,128)(2,1)S(1)}, bf16[256,128]{0,1:T(8,128)(2,1)S(1)}, u32[]{:S(2)}, u32[]{:S(2)}) collective-permute-start(bf16[256,128]{0,1:T(8,128)(2,1)S(1)} %pad.4), channel_id=1, source_target_pairs={{0,8},{4,12},{8,16},{12,20},{16,24},{20,28},{24,0},{28,4},{1,9},{5... | collective-permute-start | bytes 196616 | tf_op jit(solution)/shard_map/ppermute | solution.py:233
  80.6 9.8 %collective-permute-start.2 = (bf16[256,128]{0,1:T(8,128)(2,1)S(1)}, bf16[256,128]{0,1:T(8,128)(2,1)S(1)}, u32[]{:S(2)}, u32[]{:S(2)}) collective-permute-start(bf16[256,128]{0,1:T(8,128)(2,1)S(1)} %pad.4), channel_id=1, source_target_pairs={{0,12},{4,16},{8,20},{12,24},{16,28},{20,0},{24,4},{28,8},{1,13},{... | collective-permute-start | bytes 196616 | tf_op jit(solution)/shard_map/ppermute | solution.py:233
  83.0 7.9 %collective-permute-start.3 = (bf16[256,128]{0,1:T(8,128)(2,1)S(1)}, bf16[256,128]{0,1:T(8,128)(2,1)S(1)}, u32[]{:S(2)}, u32[]{:S(2)}) collective-permute-start(bf16[256,128]{0,1:T(8,128)(2,1)S(1)} %pad.4), channel_id=1, source_target_pairs={{0,16},{4,20},{8,24},{12,28},{16,0},{20,4},{24,8},{28,12},{1,17},{... | collective-permute-start | bytes 196616 | tf_op jit(solution)/shard_map/ppermute | solution.py:233
  84.5 8.9 %collective-permute-start.4 = (bf16[256,128]{0,1:T(8,128)(2,1)S(1)}, bf16[256,128]{0,1:T(8,128)(2,1)S(1)}, u32[]{:S(2)}, u32[]{:S(2)}) collective-permute-start(bf16[256,128]{0,1:T(8,128)(2,1)S(1)} %pad.4), channel_id=1, source_target_pairs={{0,20},{4,24},{8,28},{12,0},{16,4},{20,8},{24,12},{28,16},{1,21},{... | collective-permute-start | bytes 196616 | tf_op jit(solution)/shard_map/ppermute | solution.py:233
  87.4 7.8 %collective-permute-start.5 = (bf16[256,128]{0,1:T(8,128)(2,1)S(1)}, bf16[256,128]{0,1:T(8,128)(2,1)S(1)}, u32[]{:S(2)}, u32[]{:S(2)}) collective-permute-start(bf16[256,128]{0,1:T(8,128)(2,1)S(1)} %pad.4), channel_id=1, source_target_pairs={{0,24},{4,28},{8,0},{12,4},{16,8},{20,12},{24,16},{28,20},{1,25},{... | collective-permute-start | bytes 196616 | tf_op jit(solution)/shard_map/ppermute | solution.py:233
  88.9 6.3 %collective-permute-start.6 = (bf16[256,128]{0,1:T(8,128)(2,1)S(1)}, bf16[256,128]{0,1:T(8,128)(2,1)S(1)}, u32[]{:S(2)}, u32[]{:S(2)}) collective-permute-start(bf16[256,128]{0,1:T(8,128)(2,1)S(1)} %pad.4), channel_id=1, source_target_pairs={{0,28},{4,0},{8,4},{12,8},{16,12},{20,16},{24,20},{28,24},{1,29},{... | collective-permute-start | bytes 196616 | tf_op jit(solution)/shard_map/ppermute | solution.py:233
  96.3 1.0 copy-start.7
  175.0 4.0 copy-start.3
  236.7 13.5 %copy-start.6 = (f32[256,4,640]{0,2,1:T(8,128)S(1)}, f32[256,4,640]{0,2,1:T(8,128)}, u32[]{:S(2)}) copy-start(f32[256,4,640]{0,2,1:T(8,128)} %copy.127) | copy-start | bytes 7864324
  250.1 1.9 copy-start.9
  250.6 1.1 copy-start.5
  257.2 1.4 copy-start.4
  270.2 4.0 copy-start.2
  274.2 84.0 %copy-start.16 = (s32[1,32]{1,0:T(1,128)S(1)}, s32[1,32]{1,0:T(1,128)}, u32[]{:S(2)}) copy-start(s32[1,32]{1,0:T(1,128)} %param.20) | copy-start | bytes 388
  274.2 158.1 %copy-start.10 = (bf16[1,256,640]{2,1,0:T(8,128)(2,1)S(1)}, bf16[1,256,640]{2,1,0:T(8,128)(2,1)}, u32[]{:S(2)}) copy-start(bf16[1,256,640]{2,1,0:T(8,128)(2,1)} %reduce-scatter.4.cloned.1.call-done) | copy-start | bytes 983044
  274.2 159.9 %copy-start.1 = (bf16[512,2560]{1,0:T(8,128)(2,1)S(1)}, bf16[512,2560]{1,0:T(8,128)(2,1)}, u32[]{:S(2)}) copy-start(bf16[512,2560]{1,0:T(8,128)(2,1)} %param.25) | copy-start | bytes 7864324
  274.3 158.1 %reduce-scatter.8.cloned.1.call-start = ((), (), s32[]{:S(2)}) async-start(), calls=%async_computation.6 | async-start | bytes 2949120 | tf_op jit(solution)/shard_map/reduce_scatter | solution.py:32
Sparse Core Ops, SparseCore 0:
  9.6 20.8 all-gather.3
  49.1 26.5 reduce-scatter.3
  79.5 87.5 all-gather.5
  274.3 83.8 reduce-scatter.5
  362.0 70.3 reduce-scatter.7
